TPU v7x, 32 devices: a whole 2x2x4 slice. The times are simulated.
32 devices in a mesh: dp: 2 (over x), row: 4 (over z), col: 4 (over y, core).
Axes of the slice: x: 2, y: 2, z: 4, core: 2. Of those that a mesh axis runs over, the one named last changes fastest.
Arguments:
- hidden: bfloat16 [8192, 896], P(('dp', 'row'), 'col'), may hold values from -6 to 6
- segments: int32 [2, 4, 4, 256], P('dp', 'col', 'row'), may hold values from 0 to 3, never falling along the last dimension, each value on 1 to 128 neighbouring positions
- attn_gain: bfloat16 [2, 896], P(None, 'col'), may hold values from 0.5 to 1.5
- qkv_weight: bfloat16 [2, 896, 1152], P(None, 'col', 'row'), as said below
- qkv_bias: bfloat16 [2, 1152], P(None, 'row'), may hold values from -3 to 3
- out_weight: bfloat16 [2, 896, 896], P(None, 'row', 'col'), may hold values from -0.09375 to 0.09375
- mlp_gain: bfloat16 [2, 896], P(None, 'col'), may hold values from 0.5 to 1.5
- gate_up_weight: bfloat16 [2, 896, 2, 4864], P(None, 'col', None, 'row'), may hold values from -0.1875 to 0.1875
- down_weight: bfloat16 [2, 4864, 896], P(None, 'row', 'col'), may hold values from -0.15625 to 0.15625
- cotangent: bfloat16 [8192, 896], P(('dp', 'row'), 'col'), may hold values from -6 to 6
Outputs:
- result: bfloat16 [8192, 896], P(('dp', 'row'), 'col')
- grad_hidden: float32 [8192, 896], P(('dp', 'row'), 'col')
- attn_gain_grad: float32 [2, 896], P(None, 'col')
- qkv_weight_grad: float32 [2, 896, 1152], P(None, 'col', 'row')
- qkv_bias_grad: float32 [2, 1152], P(None, 'row')
- out_weight_grad: float32 [2, 896, 896], P(None, 'row', 'col')
- mlp_gain_grad: float32 [2, 896], P(None, 'col')
- gate_up_grad: float32 [2, 896, 2, 4864], P(None, 'col', None, 'row')
- down_grad: float32 [2, 4864, 896], P(None, 'row', 'col')
Inputs may be any that keep to these rules, and one draw needn't show every extreme that they name: `segments`: along each packed sequence of 256 tokens the numbers never fall; each number covers at most 128 tokens, and some covers exactly that many. `qkv_weight`: entries lie within 48 * 896 ** -0.5 in magnitude.
All inputs are finite; a program needn't handle non-finite values.
Results may differ from a plain program's by a relative error of at most 0.023.
Values may be sent and summed in bfloat16 or wider, within the bound.
A program may use at most 256 MiB of HBM per device.

v0:
```python
import math
import jax
import jax.numpy as jnp
from jax import lax
from jax.sharding import PartitionSpec as P

D = 896
HEADS = 14
KV = 2
HEAD = 64
LAYERS = 2
norm_eps = 1e-06
rope_base = 1000000.0


def as_sent(x):

    def short(part):
        return part.astype(jnp.bfloat16) if part.dtype == jnp.float32 else part

    return jax.tree.map(short, x)


def multiply(left_rows, right_matrix, transposed):
    if transposed:
        return lax.dot_general(
            left_rows, right_matrix, (((1,), (1,)), ((), ())), preferred_element_type=jnp.float32
        )
    return jnp.dot(left_rows, right_matrix, preferred_element_type=jnp.float32)


def inner_rows(left_rows, right_rows):
    return lax.dot_general(
        left_rows, right_rows, (((0,), (0,)), ((), ())), preferred_element_type=jnp.float32
    )


def gather_rows(values):
    return lax.all_gather(values, "row", axis=0, tiled=True)


def gather_cols(values):
    return lax.all_gather(values, "col", axis=0, tiled=True)


def reduce_cols(left_rows, right_matrix, transposed):
    share_rows = left_rows.shape[0] // lax.axis_size("col")

    def block_term(start_row, row_count):
        return multiply(left_rows, right_matrix, transposed)

    return lax.psum_scatter(
        block_term(jnp.int32(0), lax.axis_size("col") * share_rows),
        "col",
        scatter_dimension=0,
        tiled=True,
    )


def reduce_rows(left_rows, right_matrix, transposed):
    share_rows = left_rows.shape[0] // lax.axis_size("row")

    def block_term(start_row, row_count):
        return multiply(left_rows, right_matrix, transposed)

    return lax.psum_scatter(
        block_term(jnp.int32(0), lax.axis_size("row") * share_rows),
        "row",
        scatter_dimension=0,
        tiled=True,
    )


def seq_layout(values):
    return lax.all_to_all(values, "row", split_axis=0, concat_axis=1, tiled=True)


def col_layout(values):
    return lax.all_to_all(values, "row", split_axis=1, concat_axis=0, tiled=True)


def width_total(values):
    return lax.psum(values, "col")


def sum_weights(grad_terms):
    return jax.tree.map(lambda part: part.astype(jnp.float32), lax.psum(as_sent(grad_terms), "dp"))


def sum_gains(grad_terms):
    return lax.psum(grad_terms, ("dp", "row"))


def norm_forward(stream, norm_gain):
    squares = width_total(jnp.sum(stream * stream, axis=1))
    inverse = lax.rsqrt(squares / D + norm_eps)
    normed = (stream * inverse[:, None] * norm_gain).astype(jnp.bfloat16)
    return (normed, inverse)


def norm_backward(stream, inverse, norm_gain, grad_normed):
    scaled = stream * inverse[:, None]
    gain_part = jnp.sum(grad_normed * scaled, axis=0)
    weighted = grad_normed * norm_gain
    inner_sum = width_total(jnp.sum(weighted * stream, axis=1))
    grad_stream = (
        weighted * inverse[:, None]
        - stream * (inverse * inverse * inverse * inner_sum / D)[:, None]
    )
    return (grad_stream, gain_part)


def rope_tables(seg_vec):
    index_all = jnp.arange(seg_vec.shape[0], dtype=jnp.int32)
    starts = jnp.concatenate([jnp.ones((1,), jnp.bool_), seg_vec[1:] != seg_vec[:-1]])
    first_idx = lax.cummax(jnp.where(starts, index_all, 0), axis=0)
    positions = (index_all - first_idx).astype(jnp.float32)
    half_dim = HEAD // 2
    freqs = rope_base ** (-(jnp.arange(half_dim, dtype=jnp.float32) * 2.0 / HEAD))
    angles = positions[:, None] * freqs[None, :]
    return (jnp.cos(angles)[:, None, :], jnp.sin(angles)[:, None, :])


def rotate(values, cosine, sine_vals):
    half_dim = values.shape[-1] // 2
    first_half = values[..., :half_dim]
    second_half = values[..., half_dim:]
    return jnp.concatenate(
        [
            first_half * cosine - second_half * sine_vals,
            second_half * cosine + first_half * sine_vals,
        ],
        axis=-1,
    )


def head_layout(qkv_seq, cosine, sine_vals):
    length = qkv_seq.shape[0]
    kv_width = KV * HEAD
    queries = rotate(
        qkv_seq[:, :D].astype(jnp.float32).reshape(length, HEADS, HEAD), cosine, sine_vals
    ).astype(jnp.bfloat16)
    keys_rot = rotate(
        qkv_seq[:, D : D + kv_width].astype(jnp.float32).reshape(length, KV, HEAD),
        cosine,
        sine_vals,
    ).astype(jnp.bfloat16)
    values_all = qkv_seq[:, D + kv_width :].reshape(length, KV, HEAD)
    block_rows = min(length, 512)
    query_blocks = queries.reshape(length // block_rows, block_rows, KV, HEADS // KV, HEAD)
    return (query_blocks, jnp.transpose(keys_rot, (1, 0, 2)), jnp.transpose(values_all, (1, 0, 2)))


def masked_scores(query_blk, keys_t, seg_blk, seg_vec, row_index):
    score_scale = 1.0 / math.sqrt(HEAD)
    col_index = jnp.arange(seg_vec.shape[0], dtype=jnp.int32)
    scores = (
        jnp.einsum("qkgd,ksd->kgqs", query_blk, keys_t, preferred_element_type=jnp.float32)
        * score_scale
    )
    allowed = (seg_blk[:, None] == seg_vec[None, :]) & (row_index[:, None] >= col_index[None, :])
    return jnp.where(allowed[None, None], scores, -1e30)


def attend_forward(qkv_seq, seg_vec, cosine, sine_vals):
    query_blocks, keys_t, values_t = head_layout(qkv_seq, cosine, sine_vals)
    num_blocks = query_blocks.shape[0]
    block_rows = query_blocks.shape[1]
    seg_blocks = seg_vec.reshape(num_blocks, block_rows)
    row_blocks = jnp.arange(seg_vec.shape[0], dtype=jnp.int32).reshape(num_blocks, block_rows)

    def one_block(inputs):
        query_blk, seg_blk, row_index = inputs
        scores = masked_scores(query_blk, keys_t, seg_blk, seg_vec, row_index)
        row_max = jnp.max(scores, axis=-1, keepdims=True)
        exp_scores = jnp.exp(scores - row_max)
        exp_total = jnp.sum(exp_scores, axis=-1, keepdims=True)
        probs = (exp_scores / exp_total).astype(jnp.bfloat16)
        output = jnp.einsum("kgqs,ksd->qkgd", probs, values_t, preferred_element_type=jnp.float32)
        return (
            output.reshape(block_rows, D).astype(jnp.bfloat16),
            (row_max + jnp.log(exp_total))[..., 0],
        )

    outputs, log_norm = lax.map(one_block, (query_blocks, seg_blocks, row_blocks))
    return (outputs.reshape(-1, D), log_norm)


def attend_backward(qkv_seq, seg_vec, cosine, sine_vals, log_norm, grad_attn):
    score_scale = 1.0 / math.sqrt(HEAD)
    query_blocks, keys_t, values_t = head_layout(qkv_seq, cosine, sine_vals)
    num_blocks = query_blocks.shape[0]
    block_rows = query_blocks.shape[1]
    length = seg_vec.shape[0]
    seg_blocks = seg_vec.reshape(num_blocks, block_rows)
    row_blocks = jnp.arange(length, dtype=jnp.int32).reshape(num_blocks, block_rows)
    grad_blocks = grad_attn.reshape(num_blocks, block_rows, KV, HEADS // KV, HEAD)

    def one_block(carry, inputs):
        grad_keys, grad_values = carry
        query_blk, grad_blk, norm_blk, seg_blk, row_index = inputs
        scores = masked_scores(query_blk, keys_t, seg_blk, seg_vec, row_index)
        probs = jnp.exp(scores - norm_blk[..., None])
        grad_probs = jnp.einsum(
            "qkgd,ksd->kgqs", grad_blk, values_t, preferred_element_type=jnp.float32
        )
        inner_sum = jnp.sum(probs * grad_probs, axis=-1, keepdims=True)
        grad_scores = (probs * (grad_probs - inner_sum)).astype(jnp.bfloat16)
        grad_values = grad_values + jnp.einsum(
            "kgqs,qkgd->ksd",
            probs.astype(jnp.bfloat16),
            grad_blk,
            preferred_element_type=jnp.float32,
        )
        grad_keys = (
            grad_keys
            + jnp.einsum(
                "kgqs,qkgd->ksd", grad_scores, query_blk, preferred_element_type=jnp.float32
            )
            * score_scale
        )
        grad_query = (
            jnp.einsum("kgqs,ksd->qkgd", grad_scores, keys_t, preferred_element_type=jnp.float32)
            * score_scale
        )
        return ((grad_keys, grad_values), grad_query)

    zero_keys = jnp.zeros(keys_t.shape, jnp.float32)
    carried, grad_query = lax.scan(
        one_block,
        (zero_keys, zero_keys),
        (query_blocks, grad_blocks, log_norm, seg_blocks, row_blocks),
    )
    grad_keys, grad_values = carried
    grad_query = rotate(grad_query.reshape(length, HEADS, HEAD), cosine, -sine_vals)
    grad_keys = rotate(jnp.transpose(grad_keys, (1, 0, 2)), cosine, -sine_vals)
    grad_values = jnp.transpose(grad_values, (1, 0, 2))
    joined = jnp.concatenate(
        [
            grad_query.reshape(length, D),
            grad_keys.reshape(length, -1),
            grad_values.reshape(length, -1),
        ],
        axis=1,
    )
    return joined.astype(jnp.bfloat16)


def silu_product(gate_part, up_part):
    return jax.nn.silu(gate_part) * up_part


def on_device(
    hidden,
    segments,
    attn_gain,
    qkv_weight,
    qkv_bias,
    out_weight,
    mlp_gain,
    gate_up_weight,
    down_weight,
    cotangent,
):
    seg_vec = segments.reshape(-1)
    cosine, sine_vals = rope_tables(seg_vec)
    stream = hidden.astype(jnp.float32)
    width_dev = gate_up_weight.shape[1]
    saved_layers = []
    for layer_no in range(LAYERS):
        gain_attn = attn_gain[layer_no].astype(jnp.float32)
        gain_mlp = mlp_gain[layer_no].astype(jnp.float32)
        normed_a, inverse_a = norm_forward(stream, gain_attn)
        gathered_a = gather_rows(normed_a)
        qkv_part = reduce_cols(gathered_a, qkv_weight[layer_no], False)
        qkv_cols = (qkv_part + qkv_bias[layer_no].astype(jnp.float32)).astype(jnp.bfloat16)
        qkv_seq = seq_layout(qkv_cols)
        attn_seq, log_norm = attend_forward(qkv_seq, seg_vec, cosine, sine_vals)
        attn_cols = col_layout(attn_seq)
        gathered_o = gather_cols(attn_cols)
        stream_mid = stream + reduce_rows(gathered_o, out_weight[layer_no], False)
        normed_m, inverse_m = norm_forward(stream_mid, gain_mlp)
        gathered_m = gather_rows(normed_m)
        gate_flat = gate_up_weight[layer_no].reshape(width_dev, -1)
        gate_up = reduce_cols(gathered_m, gate_flat, False)
        ff_dev = gate_up.shape[1] // 2
        act_vals = silu_product(gate_up[:, :ff_dev], gate_up[:, ff_dev:]).astype(jnp.bfloat16)
        gathered_h = gather_cols(act_vals)
        stream_next = stream_mid + reduce_rows(gathered_h, down_weight[layer_no], False)
        stored = (gathered_a, gathered_o, gathered_m, gathered_h)
        saved_layers.append(
            (stream, inverse_a, qkv_seq, log_norm, stream_mid, inverse_m, gate_up, stored)
        )
        stream = stream_next
    outcome = stream.astype(jnp.bfloat16)
    grad_stream = cotangent.astype(jnp.float32)
    weight_list = []
    gain_list = []
    for layer_no in reversed(range(LAYERS)):
        stream_in, inverse_a, qkv_seq, log_norm, stream_mid, inverse_m, gate_up, stored = (
            saved_layers[layer_no]
        )
        gain_attn = attn_gain[layer_no].astype(jnp.float32)
        gain_mlp = mlp_gain[layer_no].astype(jnp.float32)
        gate_flat = gate_up_weight[layer_no].reshape(width_dev, -1)
        ff_dev = gate_up.shape[1] // 2
        grad_down = grad_stream.astype(jnp.bfloat16)
        gathered_d = gather_rows(grad_down)
        grad_act = reduce_cols(gathered_d, down_weight[layer_no], True)
        gathered_h = stored[3]
        w_down_grad = inner_rows(gathered_h, gathered_d)
        silu_out, silu_back = jax.vjp(silu_product, gate_up[:, :ff_dev], gate_up[:, ff_dev:])
        grad_gate, grad_up = silu_back(grad_act)
        grad_gu = jnp.concatenate([grad_gate, grad_up], axis=1).astype(jnp.bfloat16)
        gathered_g = gather_cols(grad_gu)
        grad_normed_m = reduce_rows(gathered_g, gate_flat, True)
        gathered_m = stored[2]
        w_gate_grad = inner_rows(gathered_m, gathered_g).reshape(width_dev, 2, ff_dev)
        grad_norm_m, gain_mlp_part = norm_backward(stream_mid, inverse_m, gain_mlp, grad_normed_m)
        grad_mid = grad_stream + grad_norm_m
        grad_out = grad_mid.astype(jnp.bfloat16)
        gathered_y = gather_rows(grad_out)
        grad_attn_cols = reduce_cols(gathered_y, out_weight[layer_no], True)
        gathered_o = stored[1]
        w_out_grad = inner_rows(gathered_o, gathered_y)
        grad_attn_seq = seq_layout(grad_attn_cols.astype(jnp.bfloat16))
        grad_qkv_seq = attend_backward(qkv_seq, seg_vec, cosine, sine_vals, log_norm, grad_attn_seq)
        grad_qkv_cols = col_layout(grad_qkv_seq)
        gathered_q = gather_cols(grad_qkv_cols)
        bias_grad = jnp.sum(gathered_q, axis=0, dtype=jnp.float32)
        grad_normed_a = reduce_rows(gathered_q, qkv_weight[layer_no], True)
        gathered_a = stored[0]
        w_qkv_grad = inner_rows(gathered_a, gathered_q)
        grad_norm_a, gain_attn_part = norm_backward(stream_in, inverse_a, gain_attn, grad_normed_a)
        grad_stream = grad_mid + grad_norm_a
        weight_terms = (w_qkv_grad, bias_grad, w_out_grad, w_gate_grad, w_down_grad)
        gain_terms = (gain_attn_part, gain_mlp_part)
        weight_list.insert(0, weight_terms)
        gain_list.insert(0, gain_terms)
    weight_stack = tuple(
        (jnp.stack([member[index_no] for member in weight_list]) for index_no in range(5))
    )
    gain_stack = tuple(
        (jnp.stack([member[index_no] for member in gain_list]) for index_no in range(2))
    )
    weight_stack = sum_weights(weight_stack)
    gain_stack = sum_gains(gain_stack)
    return (
        outcome,
        grad_stream,
        gain_stack[0],
        weight_stack[0],
        weight_stack[1],
        weight_stack[2],
        gain_stack[1],
        weight_stack[3],
        weight_stack[4],
    )


def solution(mesh):
    in_specs = (
        P(("dp", "row"), "col"),
        P("dp", "col", "row", None),
        P(None, "col"),
        P(None, "col", "row"),
        P(None, "row"),
        P(None, "row", "col"),
        P(None, "col"),
        P(None, "col", None, "row"),
        P(None, "row", "col"),
        P(("dp", "row"), "col"),
    )
    out_specs = (
        P(("dp", "row"), "col"),
        P(("dp", "row"), "col"),
        P(None, "col"),
        P(None, "col", "row"),
        P(None, "row"),
        P(None, "row", "col"),
        P(None, "col"),
        P(None, "col", None, "row"),
        P(None, "row", "col"),
    )
    return jax.shard_map(
        on_device, mesh=mesh, in_specs=in_specs, out_specs=out_specs, check_vma=False
    )
```

profile of v0, /device:TPU:0, one launch (start us, length us, event | category | flops | bytes accessed | tf_op | source)
XLA Modules:
  0.0 2898.2 jit_solution(12900651117420374474)
XLA Ops:
  19.5 41.7 %all-gather.17.cloned.1.call-done = bf16[4096,224]{0,1:T(8,128)(2,1)} async-done(((bf16[1024,224]{0,1:T(8,128)(2,1)}), bf16[4096,224]{0,1:T(8,128)(2,1)}) %all-gather.17.cloned.1.call-update) | async-done | bytes 1835024 | tf_op jit(solution)/shard_map/all_gather | solution.py:39
  67.1 45.5 %reduce-scatter.17.cloned.1.call-done = f32[1024,288]{0,1:T(8,128)} async-done(((f32[4096,288]{0,1:T(8,128)}), f32[1024,288]{0,1:T(8,128)}) %reduce-scatter.17.cloned.1.call-update) | async-done | bytes 1179664 | tf_op jit(solution)/shard_map/reduce_scatter | solution.py:52
  178.8 68.0 %reduce-scatter.19.cloned.1.call-done = f32[1024,224]{0,1:T(8,128)} async-done(((f32[4096,224]{0,1:T(8,128)}), f32[1024,224]{0,1:T(8,128)}) %reduce-scatter.19.cloned.1.call-update) | async-done | bytes 917520 | tf_op jit(solution)/shard_map/reduce_scatter | solution.py:66
  314.3 268.9 %reduce-scatter.21.cloned.1.call-done = f32[1024,2432]{1,0:T(8,128)} async-done(((f32[4096,2432]{1,0:T(8,128)}), f32[1024,2432]{1,0:T(8,128)}) %reduce-scatter.21.cloned.1.call-update) | async-done | bytes 9961488 | tf_op jit(solution)/shard_map/reduce_scatter | solution.py:52
  589.4 70.3 %all-gather.23.cloned.1.call-done = bf16[4096,1216]{1,0:T(8,128)(2,1)} async-done(((bf16[1024,1216]{1,0:T(8,128)(2,1)}), bf16[4096,1216]{1,0:T(8,128)(2,1)}) %all-gather.23.cloned.1.call-update) | async-done | bytes 9961488 | tf_op jit(solution)/shard_map/all_gather | solution.py:43
  668.7 68.6 %reduce-scatter.23.cloned.1.call-done = f32[1024,224]{0,1:T(8,128)} async-done(((f32[4096,224]{0,1:T(8,128)}), f32[1024,224]{0,1:T(8,128)}) %reduce-scatter.23.cloned.1.call-update) | async-done | bytes 917520 | tf_op jit(solution)/shard_map/reduce_scatter | solution.py:66
  745.9 41.4 %all-gather.25.cloned.1.call-done = bf16[4096,224]{0,1:T(8,128)(2,1)} async-done(((bf16[1024,224]{0,1:T(8,128)(2,1)}), bf16[4096,224]{0,1:T(8,128)(2,1)}) %all-gather.25.cloned.1.call-update) | async-done | bytes 1835024 | tf_op jit(solution)/shard_map/all_gather | solution.py:39
  791.9 46.7 %reduce-scatter.25.cloned.1.call-done = f32[1024,288]{0,1:T(8,128)} async-done(((f32[4096,288]{0,1:T(8,128)}), f32[1024,288]{0,1:T(8,128)}) %reduce-scatter.25.cloned.1.call-update) | async-done | bytes 1179664 | tf_op jit(solution)/shard_map/reduce_scatter | solution.py:52
  903.1 67.9 %reduce-scatter.27.cloned.1.call-done = f32[1024,224]{0,1:T(8,128)} async-done(((f32[4096,224]{0,1:T(8,128)}), f32[1024,224]{0,1:T(8,128)}) %reduce-scatter.27.cloned.1.call-update) | async-done | bytes 917520 | tf_op jit(solution)/shard_map/reduce_scatter | solution.py:66
  1083.8 124.4 %reduce-scatter.33.cloned.1.call-done = f32[1024,1216]{1,0:T(8,128)} async-done(((f32[4096,1216]{1,0:T(8,128)}), f32[1024,1216]{1,0:T(8,128)}) %reduce-scatter.33.cloned.1.call-update) | async-done | bytes 4980752 | tf_op jit(solution)/shard_map/reduce_scatter | solution.py:52
  1208.2 272.7 %reduce-scatter.29.cloned.1.call-done = f32[1024,2432]{1,0:T(8,128)} async-done(((f32[4096,2432]{1,0:T(8,128)}), f32[1024,2432]{1,0:T(8,128)}) %reduce-scatter.29.cloned.1.call-update) | async-done | bytes 9961488 | tf_op jit(solution)/shard_map/reduce_scatter | solution.py:52
  1493.0 125.9 %all-gather.35.cloned.1.call-done = bf16[4096,2432]{1,0:T(8,128)(2,1)} async-done(((bf16[1024,2432]{1,0:T(8,128)(2,1)}), bf16[4096,2432]{1,0:T(8,128)(2,1)}) %all-gather.35.cloned.1.call-update) | async-done | bytes 19922960 | tf_op jit(solution)/shard_map/all_gather | solution.py:43
  1633.8 68.6 %reduce-scatter.35.cloned.1.call-done = f32[1024,224]{0,1:T(8,128)} async-done(((f32[4096,224]{0,1:T(8,128)}), f32[1024,224]{0,1:T(8,128)}) %reduce-scatter.35.cloned.1.call-update) | async-done | bytes 917520 | tf_op jit(solution)/shard_map/reduce_scatter | solution.py:66
  1714.7 41.4 %all-gather.37.cloned.1.call-done = bf16[4096,224]{0,1:T(8,128)(2,1)} async-done(((bf16[1024,224]{0,1:T(8,128)(2,1)}), bf16[4096,224]{0,1:T(8,128)(2,1)}) %all-gather.37.cloned.1.call-update) | async-done | bytes 1835024 | tf_op jit(solution)/shard_map/all_gather | solution.py:39
  1873.1 67.0 %all-gather.31.cloned.1.call-done = bf16[4096,1216]{1,0:T(8,128)(2,1)} async-done(((bf16[1024,1216]{1,0:T(8,128)(2,1)}), bf16[4096,1216]{1,0:T(8,128)(2,1)}) %all-gather.31.cloned.1.call-update) | async-done | bytes 9961488 | tf_op jit(solution)/shard_map/all_gather | solution.py:43
  1949.4 62.3 %reduce-scatter.39.cloned.1.call-done = f32[1024,224]{0,1:T(8,128)} async-done(((f32[4096,224]{0,1:T(8,128)}), f32[1024,224]{0,1:T(8,128)}) %reduce-scatter.39.cloned.1.call-update) | async-done | bytes 917520 | tf_op jit(solution)/shard_map/reduce_scatter | solution.py:66
  2019.2 63.4 %reduce-scatter.31.cloned.1.call-done = f32[1024,224]{0,1:T(8,128)} async-done(((f32[4096,224]{0,1:T(8,128)}), f32[1024,224]{0,1:T(8,128)}) %reduce-scatter.31.cloned.1.call-update) | async-done | bytes 917520 | tf_op jit(solution)/shard_map/reduce_scatter | solution.py:66
  2086.2 41.7 %all-gather.41.cloned.1.call-done = bf16[4096,224]{0,1:T(8,128)(2,1)} async-done(((bf16[1024,224]{0,1:T(8,128)(2,1)}), bf16[4096,224]{0,1:T(8,128)(2,1)}) %all-gather.41.cloned.1.call-update) | async-done | bytes 1835024 | tf_op jit(solution)/shard_map/all_gather | solution.py:39
  2139.6 149.3 %reduce-scatter.41.cloned.1.call-done = f32[1024,1216]{1,0:T(8,128)} async-done(((f32[4096,1216]{1,0:T(8,128)}), f32[1024,1216]{1,0:T(8,128)}) %reduce-scatter.41.cloned.1.call-update) | async-done | bytes 4980752 | tf_op jit(solution)/shard_map/reduce_scatter | solution.py:52
  2299.8 125.9 %all-gather.43.cloned.1.call-done = bf16[4096,2432]{1,0:T(8,128)(2,1)} async-done(((bf16[1024,2432]{1,0:T(8,128)(2,1)}), bf16[4096,2432]{1,0:T(8,128)(2,1)}) %all-gather.43.cloned.1.call-update) | async-done | bytes 19922960 | tf_op jit(solution)/shard_map/all_gather | solution.py:43
  2438.0 68.6 %reduce-scatter.43.cloned.1.call-done = f32[1024,224]{0,1:T(8,128)} async-done(((f32[4096,224]{0,1:T(8,128)}), f32[1024,224]{0,1:T(8,128)}) %reduce-scatter.43.cloned.1.call-update) | async-done | bytes 917520 | tf_op jit(solution)/shard_map/reduce_scatter | solution.py:66
  2516.8 41.4 %all-gather.45.cloned.1.call-done = bf16[4096,224]{0,1:T(8,128)(2,1)} async-done(((bf16[1024,224]{0,1:T(8,128)(2,1)}), bf16[4096,224]{0,1:T(8,128)(2,1)}) %all-gather.45.cloned.1.call-update) | async-done | bytes 1835024 | tf_op jit(solution)/shard_map/all_gather | solution.py:39
  2698.3 90.3 %all-reduce.4.cloned.1.call-done = (bf16[2,224,288]{1,2,0:T(8,128)(2,1)}, bf16[2,224,224]{2,1,0:T(8,128)(2,1)}, bf16[2,224,2,1216]{3,2,1,0:T(2,128)(2,1)}, bf16[2,1216,224]{1,2,0:T(8,128)(2,1)}) async-done(((bf16[2,224,288]{1,2,0:T(8,128)(2,1)}, bf16[2,224,224]{2,1,0:T(8,128)(2,1)}, bf16[2,224,2,1216]{3,2,1,0:T(2,128)(2,1)}, bf16[2,1216,224]{1,2,0:T(8,128)(2,1)}), (bf16[2,224,288]{1,2,0:T(8,128)(2,1)}, ...) | async-done | bytes 3727376 | tf_op jit(solution)/shard_map/psum | solution.py:87
  2797.3 62.1 %reduce-scatter.47.cloned.1.call-done = f32[1024,224]{0,1:T(8,128)} async-done(((f32[4096,224]{0,1:T(8,128)}), f32[1024,224]{0,1:T(8,128)}) %reduce-scatter.47.cloned.1.call-update) | async-done | bytes 917520 | tf_op jit(solution)/shard_map/reduce_scatter | solution.py:66
  (405 shorter events, 758.1 us)
Async XLA Ops:
  19.5 93.1 %reduce-scatter.17.cloned.1.call-start = ((), (), s32[]{:S(2)}) async-start(), calls=%async_computation.25 | async-start | bytes 5898240 | tf_op jit(solution)/shard_map/reduce_scatter | solution.py:52
  178.1 118.7 %all-gather.21.cloned.1.call-start = ((), (), s32[]{:S(2)}) async-start(), calls=%async_computation.28 | async-start | bytes 2293760 | tf_op jit(solution)/shard_map/all_gather | solution.py:39
  255.3 327.9 %reduce-scatter.21.cloned.1.call-start = ((), (), s32[]{:S(2)}) async-start(), calls=%async_computation.29 | async-start | bytes 49807360 | tf_op jit(solution)/shard_map/reduce_scatter | solution.py:52
  314.1 345.6 %all-gather.23.cloned.1.call-start = ((), (), s32[]{:S(2)}) async-start(), calls=%async_computation.30 | async-start | bytes 13107200 | tf_op jit(solution)/shard_map/all_gather | solution.py:43
  589.3 148.1 %reduce-scatter.23.cloned.1.call-start = ((), (), s32[]{:S(2)}) async-start(), calls=%async_computation.31 | async-start | bytes 4587520 | tf_op jit(solution)/shard_map/reduce_scatter | solution.py:66
  668.7 118.7 %all-gather.25.cloned.1.call-start = ((), (), s32[]{:S(2)}) async-start(), calls=%async_computation.32 | async-start | bytes 2293760 | tf_op jit(solution)/shard_map/all_gather | solution.py:39
  791.8 106.4 %all-gather.27.cloned.1.call-start = ((), (), s32[]{:S(2)}) async-start(), calls=%async_computation.34 | async-start | bytes 2293760 | tf_op jit(solution)/shard_map/all_gather | solution.py:43
  902.3 111.9 %all-gather.33.cloned.1.call-start = ((), (), s32[]{:S(2)}) async-start(), calls=%async_computation.40 | async-start | bytes 2293760 | tf_op jit(solution)/shard_map/all_gather | solution.py:39
  903.1 153.3 %all-gather.29.cloned.1.call-start = ((), (), s32[]{:S(2)}) async-start(), calls=%async_computation.36 | async-start | bytes 2293760 | tf_op jit(solution)/shard_map/all_gather | solution.py:39
  979.4 228.8 %reduce-scatter.33.cloned.1.call-start = ((), (), s32[]{:S(2)}) async-start(), calls=%async_computation.41 | async-start | bytes 26214400 | tf_op jit(solution)/shard_map/reduce_scatter | solution.py:52
  1026.2 454.7 %reduce-scatter.29.cloned.1.call-start = ((), (), s32[]{:S(2)}) async-start(), calls=%async_computation.37 | async-start | bytes 49807360 | tf_op jit(solution)/shard_map/reduce_scatter | solution.py:52
  1083.8 535.1 %all-gather.35.cloned.1.call-start = ((), (), s32[]{:S(2)}) async-start(), calls=%async_computation.42 | async-start | bytes 24903680 | tf_op jit(solution)/shard_map/all_gather | solution.py:43
  1493.0 209.4 %reduce-scatter.35.cloned.1.call-start = ((), (), s32[]{:S(2)}) async-start(), calls=%async_computation.43 | async-start | bytes 4587520 | tf_op jit(solution)/shard_map/reduce_scatter | solution.py:66
  1633.7 122.4 %all-gather.37.cloned.1.call-start = ((), (), s32[]{:S(2)}) async-start(), calls=%async_computation.44 | async-start | bytes 2293760 | tf_op jit(solution)/shard_map/all_gather | solution.py:39
  1846.1 94.1 %all-gather.31.cloned.1.call-start = ((), (), s32[]{:S(2)}) async-start(), calls=%async_computation.38 | async-start | bytes 13107200 | tf_op jit(solution)/shard_map/all_gather | solution.py:43
  1846.8 164.8 %reduce-scatter.39.cloned.1.call-start = ((), (), s32[]{:S(2)}) async-start(), calls=%async_computation.47 | async-start | bytes 4587520 | tf_op jit(solution)/shard_map/reduce_scatter | solution.py:66
  1873.1 209.6 %reduce-scatter.31.cloned.1.call-start = ((), (), s32[]{:S(2)}) async-start(), calls=%async_computation.39 | async-start | bytes 4587520 | tf_op jit(solution)/shard_map/reduce_scatter | solution.py:66
  1949.3 178.5 %all-gather.41.cloned.1.call-start = ((), (), s32[]{:S(2)}) async-start(), calls=%async_computation.48 | async-start | bytes 2293760 | tf_op jit(solution)/shard_map/all_gather | solution.py:39
  2086.1 202.8 %reduce-scatter.41.cloned.1.call-start = ((), (), s32[]{:S(2)}) async-start(), calls=%async_computation.49 | async-start | bytes 26214400 | tf_op jit(solution)/shard_map/reduce_scatter | solution.py:52
  2139.4 286.2 %all-gather.43.cloned.1.call-start = ((), (), s32[]{:S(2)}) async-start(), calls=%async_computation.50 | async-start | bytes 24903680 | tf_op jit(solution)/shard_map/all_gather | solution.py:43
  2299.7 207.0 %reduce-scatter.43.cloned.1.call-start = ((), (), s32[]{:S(2)}) async-start(), calls=%async_computation.51 | async-start | bytes 4587520 | tf_op jit(solution)/shard_map/reduce_scatter | solution.py:66
  2438.0 120.3 %all-gather.45.cloned.1.call-start = ((), (), s32[]{:S(2)}) async-start(), calls=%async_computation.52 | async-start | bytes 2293760 | tf_op jit(solution)/shard_map/all_gather | solution.py:39
  2651.0 137.6 %all-reduce.4.cloned.1.call-start = ((), (), s32[]{:S(2)}) async-start(), calls=%async_computation.56 | async-start | bytes 7929856 | tf_op jit(solution)/shard_map/psum | solution.py:87
  2684.6 174.7 %reduce-scatter.47.cloned.1.call-start = ((), (), s32[]{:S(2)}) async-start(), calls=%async_computation.55 | async-start | bytes 4587520 | tf_op jit(solution)/shard_map/reduce_scatter | solution.py:66
  (98 other events, 6673.6 us)
Sparse Core Ops, SparseCore 0:
  19.6 41.6 all-gather.16
  66.0 46.5 reduce-scatter.16
  178.3 68.5 reduce-scatter.18
  255.4 41.3 all-gather.20
  314.2 268.9 reduce-scatter.20
  589.5 70.1 all-gather.22
  668.8 68.5 reduce-scatter.22
  792.0 46.5 reduce-scatter.24
  902.4 68.5 reduce-scatter.26
  972.6 41.5 all-gather.32
  1058.8 149.3 reduce-scatter.32
  1210.7 270.1 reduce-scatter.28
  1493.1 125.7 all-gather.34
  1633.8 68.5 reduce-scatter.34
  1870.0 70.1 all-gather.30
  1943.1 68.5 reduce-scatter.38
  2013.8 68.8 reduce-scatter.30
  2086.2 41.5 all-gather.40
  2139.5 149.3 reduce-scatter.40
  2299.8 125.7 all-gather.42
  2438.1 68.5 reduce-scatter.42
  2516.9 41.3 all-gather.44
  2684.7 103.7 all-reduce.3
  2790.7 68.5 reduce-scatter.46
  (9 shorter events, 287.1 us)
where the time goes:
time: 2910 us; the launch traced here: 2900 us
  waiting for transfers between devices  2400 us (82%)
  matrix products  204 us (7%)
  blocking collectives  147 us (5%)
  other arithmetic  90.5 us (3%)
    reduce_scatter x8, waiting for transfers between devices, reduce_cols(): lax.psum_scatter(block_term(jnp.int32(0), lax.axis_size('col') * share_ro...  988 us
    reduce_scatter x8, waiting for transfers between devices, reduce_rows(): lax.psum_scatter(block_term(jnp.int32(0), lax.axis_size('row') * share_ro...  530 us
    all_gather x8, waiting for transfers between devices, gather_cols(): return lax.all_gather(values, 'col', axis=0, tiled=True)  449 us
    all_gather x8, waiting for transfers between devices, gather_rows(): return lax.all_gather(values, 'row', axis=0, tiled=True)  306 us
    psum x1, waiting for transfers between devices, sum_weights(): lax.psum(as_sent(grad_terms), 'dp')  90.3 us
    dot_general x8, matrix products, multiply(): return jnp.dot(left_rows, right_matrix, preferred_element_type=jnp.float32)  79.7 us
    dot_general x8, matrix products, multiply(): lax.dot_general(left_rows, right_matrix, (((1,), (1,)), ((), ())), prefer...  67.9 us
  transfers between devices with their start and end apart: 37, of which 35 were waited for; matrix products, arithmetic and copies ran while one was open for 5% of the time, Pallas kernels for 0%

commit v1 on v0

--- a/solution.py
+++ b/solution.py
@@ -36,7 +36,34 @@
 
 
 def gather_rows(values):
-    return lax.all_gather(values, "row", axis=0, tiled=True)
+
+    def expand_slots(matrix, axis_tag):
+        inter, spare, all_rows = (lax.psum(1, axis_tag), lax.axis_index(axis_tag), matrix.shape[0])
+        y2 = moved = matrix
+        block_last = lax.dynamic_update_slice_in_dim(
+            jnp.zeros(
+                [dev * inter if ii == 0 else dev for ii, dev in enumerate(matrix.shape)],
+                matrix.dtype,
+            ),
+            matrix,
+            spare * all_rows,
+            axis=0,
+        )
+        for i0 in range(1, inter // 2 + 1):
+            y2 = lax.ppermute(y2, axis_tag, perm=[(ii, (ii + 1) % inter) for ii in range(inter)])
+            block_last = lax.dynamic_update_slice_in_dim(
+                block_last, y2, (spare - i0) % inter * all_rows, axis=0
+            )
+            if 2 * i0 < inter:
+                moved = lax.ppermute(
+                    moved, axis_tag, [(ii, (ii - 1) % inter) for ii in range(inter)]
+                )
+                block_last = lax.dynamic_update_slice_in_dim(
+                    block_last, moved, (spare + i0) % inter * all_rows, axis=0
+                )
+        return block_last
+
+    return expand_slots(values, "row")
 
 
 def gather_cols(values):

time: 2910 us -> 2790 us (0.959)
  waiting for transfers between devices: 2400 us -> 2200 us
  starting transfers between devices: 19.7 us -> 97.4 us
    all_gather x8 -> x0, waiting for transfers between devices: 306 us -> none  [gather_rows(): return lax.all_gather(values, 'row', axis=0, tiled=True)]
    ppermute x0 -> x24, waiting for transfers between devices: none -> 201 us  [the longest x16 171 us: expand_slots(): lax.ppermute(y2, axis_tag, perm=[(ii, (ii + 1) % inter) for ii in range(i...]
    ppermute x0 -> x24, starting transfers between devices: none -> 78.1 us  [the longest x16 59.4 us: expand_slots(): lax.ppermute(y2, axis_tag, perm=[(ii, (ii + 1) % inter) for ii in range(i...]
    reduce_scatter x8, waiting for transfers between devices: 530 us -> 487 us  [reduce_rows(): lax.psum_scatter(block_term(jnp.int32(0), lax.axis_size('row') * share_ro...]
    reduce_scatter x8, waiting for transfers between devices: 988 us -> 952 us  [reduce_cols(): lax.psum_scatter(block_term(jnp.int32(0), lax.axis_size('col') * share_ro...]
  transfers between devices with their start and end apart: 37 -> 53, of which waited for: 35 -> 50; matrix products, arithmetic and copies ran while one was open for 5% -> 5% of each run, Pallas kernels for 0% -> 0%
where the time goes in v1:
time: 2790 us; the launch traced here: 2780 us
  waiting for transfers between devices  2200 us (79%)
  matrix products  184 us (7%)
  blocking collectives  147 us (5%)
  starting transfers between devices  97.4 us (3%)
  other arithmetic  86.7 us (3%)
  local copies, waits for them, and re-layouts  49.9 us (2%)
    reduce_scatter x8, waiting for transfers between devices, reduce_cols(): lax.psum_scatter(block_term(jnp.int32(0), lax.axis_size('col') * share_ro...  952 us
    reduce_scatter x8, waiting for transfers between devices, reduce_rows(): lax.psum_scatter(block_term(jnp.int32(0), lax.axis_size('row') * share_ro...  487 us
    all_gather x8, waiting for transfers between devices, gather_cols(): return lax.all_gather(values, 'col', axis=0, tiled=True)  439 us
    ppermute x16, waiting for transfers between devices, expand_slots(): lax.ppermute(y2, axis_tag, perm=[(ii, (ii + 1) % inter) for ii in range(i...  171 us
    psum x1, waiting for transfers between devices, sum_weights(): lax.psum(as_sent(grad_terms), 'dp')  89.3 us
    dot_general x8, matrix products, multiply(): return jnp.dot(left_rows, right_matrix, preferred_element_type=jnp.float32)  65.5 us
    ppermute x16, starting transfers between devices, expand_slots(): lax.ppermute(y2, axis_tag, perm=[(ii, (ii + 1) % inter) for ii in range(i...  59.4 us
    dot_general x8, matrix products, multiply(): lax.dot_general(left_rows, right_matrix, (((1,), (1,)), ((), ())), prefer...  58.7 us
  transfers between devices with their start and end apart: 53, of which 50 were waited for; matrix products, arithmetic and copies ran while one was open for 5% of the time, Pallas kernels for 0%

profile of v1, /device:TPU:0, one launch (start us, length us, event | category | flops | bytes accessed | tf_op | source)
XLA Modules:
  0.0 2781.8 jit_solution(11809535819020160463)
XLA Ops:
  57.0 46.1 %reduce-scatter.17.cloned.1.call-done = f32[1024,288]{0,1:T(8,128)} async-done(((f32[4096,288]{0,1:T(8,128)}), f32[1024,288]{0,1:T(8,128)}) %reduce-scatter.17.cloned.1.call-update) | async-done | bytes 1179664 | tf_op jit(solution)/shard_map/reduce_scatter | solution.py:79
  169.5 68.0 %reduce-scatter.19.cloned.1.call-done = f32[1024,224]{0,1:T(8,128)} async-done(((f32[4096,224]{0,1:T(8,128)}), f32[1024,224]{0,1:T(8,128)}) %reduce-scatter.19.cloned.1.call-update) | async-done | bytes 917520 | tf_op jit(solution)/shard_map/reduce_scatter | solution.py:93
  296.8 269.0 %reduce-scatter.21.cloned.1.call-done = f32[1024,2432]{1,0:T(8,128)} async-done(((f32[4096,2432]{1,0:T(8,128)}), f32[1024,2432]{1,0:T(8,128)}) %reduce-scatter.21.cloned.1.call-update) | async-done | bytes 9961488 | tf_op jit(solution)/shard_map/reduce_scatter | solution.py:79
  571.9 70.3 %all-gather.11.cloned.1.call-done = bf16[4096,1216]{1,0:T(8,128)(2,1)} async-done(((bf16[1024,1216]{1,0:T(8,128)(2,1)}), bf16[4096,1216]{1,0:T(8,128)(2,1)}) %all-gather.11.cloned.1.call-update) | async-done | bytes 9961488 | tf_op jit(solution)/shard_map/all_gather | solution.py:70
  651.3 68.6 %reduce-scatter.23.cloned.1.call-done = f32[1024,224]{0,1:T(8,128)} async-done(((f32[4096,224]{0,1:T(8,128)}), f32[1024,224]{0,1:T(8,128)}) %reduce-scatter.23.cloned.1.call-update) | async-done | bytes 917520 | tf_op jit(solution)/shard_map/reduce_scatter | solution.py:93
  765.6 46.6 %reduce-scatter.25.cloned.1.call-done = f32[1024,288]{0,1:T(8,128)} async-done(((f32[4096,288]{0,1:T(8,128)}), f32[1024,288]{0,1:T(8,128)}) %reduce-scatter.25.cloned.1.call-update) | async-done | bytes 1179664 | tf_op jit(solution)/shard_map/reduce_scatter | solution.py:79
  813.7 20.1 all_to_all.135
  948.5 23.7 reduce-scatter.27.cloned.1.call-done
  1035.5 88.7 %reduce-scatter.33.cloned.1.call-done = f32[1024,1216]{1,0:T(8,128)} async-done(((f32[4096,1216]{1,0:T(8,128)}), f32[1024,1216]{1,0:T(8,128)}) %reduce-scatter.33.cloned.1.call-update) | async-done | bytes 4980752 | tf_op jit(solution)/shard_map/reduce_scatter | solution.py:79
  1124.2 272.8 %reduce-scatter.29.cloned.1.call-done = f32[1024,2432]{1,0:T(8,128)} async-done(((f32[4096,2432]{1,0:T(8,128)}), f32[1024,2432]{1,0:T(8,128)}) %reduce-scatter.29.cloned.1.call-update) | async-done | bytes 9961488 | tf_op jit(solution)/shard_map/reduce_scatter | solution.py:79
  1412.6 64.0 %all-gather.15.cloned.1.call-done = bf16[4096,1216]{1,0:T(8,128)(2,1)} async-done(((bf16[1024,1216]{1,0:T(8,128)(2,1)}), bf16[4096,1216]{1,0:T(8,128)(2,1)}) %all-gather.15.cloned.1.call-update) | async-done | bytes 9961488 | tf_op jit(solution)/shard_map/all_gather | solution.py:70
  1486.3 117.7 %all-gather.17.cloned.1.call-done = bf16[4096,2432]{1,0:T(8,128)(2,1)} async-done(((bf16[1024,2432]{1,0:T(8,128)(2,1)}), bf16[4096,2432]{1,0:T(8,128)(2,1)}) %all-gather.17.cloned.1.call-update) | async-done | bytes 19922960 | tf_op jit(solution)/shard_map/all_gather | solution.py:70
  1618.9 55.8 %reduce-scatter.31.cloned.1.call-done = f32[1024,224]{0,1:T(8,128)} async-done(((f32[4096,224]{0,1:T(8,128)}), f32[1024,224]{0,1:T(8,128)}) %reduce-scatter.31.cloned.1.call-update) | async-done | bytes 917520 | tf_op jit(solution)/shard_map/reduce_scatter | solution.py:93
  1674.7 71.6 %reduce-scatter.35.cloned.1.call-done = f32[1024,224]{0,1:T(8,128)} async-done(((f32[4096,224]{0,1:T(8,128)}), f32[1024,224]{0,1:T(8,128)}) %reduce-scatter.35.cloned.1.call-update) | async-done | bytes 917520 | tf_op jit(solution)/shard_map/reduce_scatter | solution.py:93
  1794.6 39.9 %reduce-scatter.37.cloned.1.call-done = f32[1024,224]{0,1:T(8,128)} async-done(((f32[4096,224]{0,1:T(8,128)}), f32[1024,224]{0,1:T(8,128)}) %reduce-scatter.37.cloned.1.call-update) | async-done | bytes 917520 | tf_op jit(solution)/shard_map/reduce_scatter | solution.py:79
  1881.1 22.3 all-gather.19.cloned.1.call-done
  1908.1 68.6 %reduce-scatter.39.cloned.1.call-done = f32[1024,224]{0,1:T(8,128)} async-done(((f32[4096,224]{0,1:T(8,128)}), f32[1024,224]{0,1:T(8,128)}) %reduce-scatter.39.cloned.1.call-update) | async-done | bytes 917520 | tf_op jit(solution)/shard_map/reduce_scatter | solution.py:93
  2030.4 149.5 %reduce-scatter.41.cloned.1.call-done = f32[1024,1216]{1,0:T(8,128)} async-done(((f32[4096,1216]{1,0:T(8,128)}), f32[1024,1216]{1,0:T(8,128)}) %reduce-scatter.41.cloned.1.call-update) | async-done | bytes 4980752 | tf_op jit(solution)/shard_map/reduce_scatter | solution.py:79
  2190.7 125.9 %all-gather.21.cloned.1.call-done = bf16[4096,2432]{1,0:T(8,128)(2,1)} async-done(((bf16[1024,2432]{1,0:T(8,128)(2,1)}), bf16[4096,2432]{1,0:T(8,128)(2,1)}) %all-gather.21.cloned.1.call-update) | async-done | bytes 19922960 | tf_op jit(solution)/shard_map/all_gather | solution.py:70
  2329.0 68.6 %reduce-scatter.43.cloned.1.call-done = f32[1024,224]{0,1:T(8,128)} async-done(((f32[4096,224]{0,1:T(8,128)}), f32[1024,224]{0,1:T(8,128)}) %reduce-scatter.43.cloned.1.call-update) | async-done | bytes 917520 | tf_op jit(solution)/shard_map/reduce_scatter | solution.py:93
  2444.5 39.2 %reduce-scatter.45.cloned.1.call-done = f32[1024,224]{0,1:T(8,128)} async-done(((f32[4096,224]{0,1:T(8,128)}), f32[1024,224]{0,1:T(8,128)}) %reduce-scatter.45.cloned.1.call-update) | async-done | bytes 917520 | tf_op jit(solution)/shard_map/reduce_scatter | solution.py:79
  2584.0 89.3 %all-reduce.4.cloned.1.call-done = (bf16[2,224,288]{1,2,0:T(8,128)(2,1)}, bf16[2,224,224]{2,1,0:T(8,128)(2,1)}, bf16[2,224,2,1216]{3,2,1,0:T(2,128)(2,1)}, bf16[2,1216,224]{1,2,0:T(8,128)(2,1)}) async-done(((bf16[2,224,288]{1,2,0:T(8,128)(2,1)}, bf16[2,224,224]{2,1,0:T(8,128)(2,1)}, bf16[2,224,2,1216]{3,2,1,0:T(2,128)(2,1)}, bf16[2,1216,224]{1,2,0:T(8,128)(2,1)}), (bf16[2,224,288]{1,2,0:T(8,128)(2,1)}, ...) | async-done | bytes 3727376 | tf_op jit(solution)/shard_map/psum | solution.py:114
  2682.0 62.2 %reduce-scatter.47.cloned.1.call-done = f32[1024,224]{0,1:T(8,128)} async-done(((f32[4096,224]{0,1:T(8,128)}), f32[1024,224]{0,1:T(8,128)}) %reduce-scatter.47.cloned.1.call-update) | async-done | bytes 917520 | tf_op jit(solution)/shard_map/reduce_scatter | solution.py:93
  2752.0 21.6 all-reduce
  (492 shorter events, 795.4 us)
Async XLA Ops:
  7.2 95.9 %reduce-scatter.17.cloned.1.call-start = ((), (), s32[]{:S(2)}) async-start(), calls=%async_computation.24 | async-start | bytes 5898240 | tf_op jit(solution)/shard_map/reduce_scatter | solution.py:79
  109.9 54.9 %all-gather.9.cloned.1.call-start = ((), (), s32[]{:S(2)}) async-start(), calls=%async_computation.25 | async-start | bytes 2293760 | tf_op jit(solution)/shard_map/all_gather | solution.py:70
  145.4 92.1 %reduce-scatter.19.cloned.1.call-start = ((), (), s32[]{:S(2)}) async-start(), calls=%async_computation.26 | async-start | bytes 4587520 | tf_op jit(solution)/shard_map/reduce_scatter | solution.py:93
  168.8 396.9 %reduce-scatter.21.cloned.1.call-start = ((), (), s32[]{:S(2)}) async-start(), calls=%async_computation.27 | async-start | bytes 49807360 | tf_op jit(solution)/shard_map/reduce_scatter | solution.py:79
  296.5 345.7 %all-gather.11.cloned.1.call-start = ((), (), s32[]{:S(2)}) async-start(), calls=%async_computation.28 | async-start | bytes 13107200 | tf_op jit(solution)/shard_map/all_gather | solution.py:70
  571.9 148.1 %reduce-scatter.23.cloned.1.call-start = ((), (), s32[]{:S(2)}) async-start(), calls=%async_computation.29 | async-start | bytes 4587520 | tf_op jit(solution)/shard_map/reduce_scatter | solution.py:93
  651.2 161.0 %reduce-scatter.25.cloned.1.call-start = ((), (), s32[]{:S(2)}) async-start(), calls=%async_computation.30 | async-start | bytes 5898240 | tf_op jit(solution)/shard_map/reduce_scatter | solution.py:79
  765.6 107.8 %all-gather.13.cloned.1.call-start = ((), (), s32[]{:S(2)}) async-start(), calls=%async_computation.31 | async-start | bytes 2293760 | tf_op jit(solution)/shard_map/all_gather | solution.py:70
  854.0 118.3 %reduce-scatter.27.cloned.1.call-start = ((), (), s32[]{:S(2)}) async-start(), calls=%async_computation.32 | async-start | bytes 4587520 | tf_op jit(solution)/shard_map/reduce_scatter | solution.py:93
  877.4 246.9 %reduce-scatter.33.cloned.1.call-start = ((), (), s32[]{:S(2)}) async-start(), calls=%async_computation.36 | async-start | bytes 26214400 | tf_op jit(solution)/shard_map/reduce_scatter | solution.py:79
  948.5 448.6 %reduce-scatter.29.cloned.1.call-start = ((), (), s32[]{:S(2)}) async-start(), calls=%async_computation.33 | async-start | bytes 49807360 | tf_op jit(solution)/shard_map/reduce_scatter | solution.py:79
  1035.5 441.2 %all-gather.15.cloned.1.call-start = ((), (), s32[]{:S(2)}) async-start(), calls=%async_computation.34 | async-start | bytes 13107200 | tf_op jit(solution)/shard_map/all_gather | solution.py:70
  1406.3 197.7 %all-gather.17.cloned.1.call-start = ((), (), s32[]{:S(2)}) async-start(), calls=%async_computation.37 | async-start | bytes 24903680 | tf_op jit(solution)/shard_map/all_gather | solution.py:70
  1412.5 262.2 %reduce-scatter.31.cloned.1.call-start = ((), (), s32[]{:S(2)}) async-start(), calls=%async_computation.35 | async-start | bytes 4587520 | tf_op jit(solution)/shard_map/reduce_scatter | solution.py:93
  1485.8 260.5 %reduce-scatter.35.cloned.1.call-start = ((), (), s32[]{:S(2)}) async-start(), calls=%async_computation.38 | async-start | bytes 4587520 | tf_op jit(solution)/shard_map/reduce_scatter | solution.py:93
  1618.9 215.7 %reduce-scatter.37.cloned.1.call-start = ((), (), s32[]{:S(2)}) async-start(), calls=%async_computation.39 | async-start | bytes 4587520 | tf_op jit(solution)/shard_map/reduce_scatter | solution.py:79
  1841.2 62.1 %all-gather.19.cloned.1.call-start = ((), (), s32[]{:S(2)}) async-start(), calls=%async_computation.40 | async-start | bytes 2949120 | tf_op jit(solution)/shard_map/all_gather | solution.py:70
  1881.0 95.7 %reduce-scatter.39.cloned.1.call-start = ((), (), s32[]{:S(2)}) async-start(), calls=%async_computation.41 | async-start | bytes 4587520 | tf_op jit(solution)/shard_map/reduce_scatter | solution.py:93
  1908.1 271.8 %reduce-scatter.41.cloned.1.call-start = ((), (), s32[]{:S(2)}) async-start(), calls=%async_computation.42 | async-start | bytes 26214400 | tf_op jit(solution)/shard_map/reduce_scatter | solution.py:79
  2030.3 286.2 %all-gather.21.cloned.1.call-start = ((), (), s32[]{:S(2)}) async-start(), calls=%async_computation.43 | async-start | bytes 24903680 | tf_op jit(solution)/shard_map/all_gather | solution.py:70
  2190.6 207.0 %reduce-scatter.43.cloned.1.call-start = ((), (), s32[]{:S(2)}) async-start(), calls=%async_computation.44 | async-start | bytes 4587520 | tf_op jit(solution)/shard_map/reduce_scatter | solution.py:93
  2328.9 154.8 %reduce-scatter.45.cloned.1.call-start = ((), (), s32[]{:S(2)}) async-start(), calls=%async_computation.45 | async-start | bytes 4587520 | tf_op jit(solution)/shard_map/reduce_scatter | solution.py:79
  2535.0 138.3 %all-reduce.4.cloned.1.call-start = ((), (), s32[]{:S(2)}) async-start(), calls=%async_computation.48 | async-start | bytes 7929856 | tf_op jit(solution)/shard_map/psum | solution.py:114
  2569.7 174.5 %reduce-scatter.47.cloned.1.call-start = ((), (), s32[]{:S(2)}) async-start(), calls=%async_computation.47 | async-start | bytes 4587520 | tf_op jit(solution)/shard_map/reduce_scatter | solution.py:93
  (129 other events, 5714.1 us)
Sparse Core Ops, SparseCore 0:
  55.8 47.1 reduce-scatter.16
  169.0 68.5 reduce-scatter.18
  296.6 269.0 reduce-scatter.20
  572.0 70.1 all-gather.10
  651.3 68.5 reduce-scatter.22
  765.7 46.5 reduce-scatter.24
  854.1 19.2 all-gather.12
  877.5 94.6 reduce-scatter.26
  974.7 149.5 reduce-scatter.32
  1126.8 270.1 reduce-scatter.28
  1406.4 70.1 all-gather.14
  1478.2 125.7 all-gather.16
  1606.2 68.5 reduce-scatter.30
  1677.5 68.8 reduce-scatter.34
  1794.7 39.7 reduce-scatter.36
  1881.1 22.1 all-gather.18
  1908.1 68.5 reduce-scatter.38
  2030.5 149.3 reduce-scatter.40
  2190.7 125.7 all-gather.20
  2329.0 68.5 reduce-scatter.42
  2443.9 39.7 reduce-scatter.44
  2535.1 24.4 all-gather.22
  2569.8 103.4 all-reduce.3
  2675.6 68.5 reduce-scatter.46
  (1 shorter events, 19.2 us)
